TPU v7x, 512 devices: a whole 4x4x16 slice. The times are simulated.
512 devices in a mesh: site: 16 (over z), patch: 32 (over x, y, core).
Axes of the slice: x: 4, y: 4, z: 16, core: 2. Of those that a mesh axis runs over, the one named last changes fastest.
Arguments:
- slip_rates: bfloat16 [512, 64, 256], P('patch', 'site'), may hold values from -6 to 6
- green_tiles: bfloat16 [16, 1024, 2, 1024], P('site', 'patch'), may hold values from -0.015625 to 0.015625
- patch_slot: int32 [512], replicated, may hold values from 0 to 1023, as said below
Outputs:
- seismograms: float32 [16, 64, 2, 1280], P('site', 'patch')
Inputs may be any that keep to these rules, and one draw needn't show every extreme that they name: The values of patch_slot all differ. Patch p belongs to owner patch_slot[p] // 32 and fills its slot patch_slot[p] % 32; each owner has 1 to 32 patches in its first slots, and some owner has exactly 32. The 16 patches p with the same p // 16 include at most 2 of any one owner, and some such group includes exactly 2 of one owner.
All inputs are finite; a program needn't handle non-finite values.
Results may differ from a plain program's by a relative error of at most 0.0003.
Values may be sent and summed in bfloat16 or wider, within the bound.
A program may use at most 64 MiB of HBM per device.

v0:
```python
import math

import jax
import jax.numpy as jnp
from jax import lax
from jax.sharding import PartitionSpec as P


def band_matrix(greens, samples):
    half_len = samples // 2
    lag_count = greens.shape[-1]
    length = samples + lag_count
    period = length + samples
    padded = jnp.pad(greens, ((0, 0), (0, 0), (half_len, period - half_len - lag_count)))
    repeated = jnp.tile(padded, (1, 1, half_len))
    shifted = repeated[..., : half_len * (period - 1)].reshape(
        greens.shape[0], greens.shape[1], half_len, period - 1
    )
    return shifted[..., : length + half_len]


def convolve_rows(slot_slips, kernels, row_count):
    item_count = slot_slips.shape[0]
    samples = slot_slips.shape[2]
    lag_count = kernels.shape[2]
    half_len = samples // 2
    length = samples + lag_count
    group_size = math.gcd(item_count, 8)
    blocks = item_count // group_size
    selected = slot_slips
    selected = selected.reshape(blocks, group_size, row_count, samples)
    kernel_blocks = kernels.reshape(blocks, group_size, 2, lag_count)

    def accumulate(running, operands):
        slip_block, kernel = operands
        band_rows = band_matrix(kernel, samples)
        running = running + jnp.einsum(
            "pvq,pcqt->vct",
            slip_block[..., :half_len],
            band_rows[..., half_len : half_len + length],
            preferred_element_type=jnp.float32,
        )
        running = running + jnp.einsum(
            "pvq,pcqt->vct",
            slip_block[..., half_len:],
            band_rows[..., :length],
            preferred_element_type=jnp.float32,
        )
        return (running, None)

    running, unused = lax.scan(
        accumulate, jnp.zeros((row_count, 2, length), jnp.float32), (selected, kernel_blocks)
    )
    return running


def route_tables(patch_slot, slot_width, sources, per_source, capacity, owner_now):
    owner_of = patch_slot // slot_width
    within = patch_slot % slot_width
    owners = owner_of.reshape(sources, per_source)
    same_owner = owners[:, :, None] == owners[:, None, :]
    earlier = lax.broadcasted_iota(jnp.int32, (per_source, per_source), 1) < lax.broadcasted_iota(
        jnp.int32, (per_source, per_source), 0
    )
    rank_of = jnp.sum((same_owner & earlier[None]).astype(jnp.int32), axis=2)
    source_code = (
        lax.broadcasted_iota(jnp.int32, (sources, per_source), 0) * capacity + rank_of
    ).reshape(-1)
    owner_code = owners * capacity + rank_of
    is_mine = owner_of == owner_now
    slot_index = lax.broadcasted_iota(jnp.int32, (slot_width, 1), 0)
    code_index = lax.broadcasted_iota(jnp.int32, (1, sources * capacity), 1)
    slot_pick = ((within[None, :] == slot_index) & is_mine[None, :]).astype(jnp.bfloat16)
    code_pick = (source_code[:, None] == code_index).astype(jnp.bfloat16)
    inbound = jnp.dot(slot_pick, code_pick, preferred_element_type=jnp.float32).astype(jnp.bfloat16)
    my_codes = lax.dynamic_index_in_dim(owner_code, owner_now, 0, keepdims=False)
    outbound = (code_index.reshape(-1, 1) == my_codes[None, :]).astype(jnp.bfloat16)
    return (inbound, outbound)


def local(slip_rates, green_tiles, patch_slot):
    sources = lax.axis_size("patch")
    per_source = slip_rates.shape[0]
    slot_width = green_tiles.shape[1]
    samples = slip_rates.shape[2]
    capacity = 2 * max(1, per_source // sources)
    own_index = lax.axis_index("patch")
    inbound, outbound = route_tables(
        patch_slot, slot_width, sources, per_source, capacity, own_index
    )
    gathered = lax.all_gather(slip_rates, "site", axis=1, tiled=True)
    flat_slip = gathered.reshape(per_source, -1)
    outgoing = jnp.dot(outbound, flat_slip, preferred_element_type=jnp.float32).astype(jnp.bfloat16)
    outgoing = outgoing.reshape(sources, capacity, flat_slip.shape[1])
    arrived = lax.all_to_all(outgoing, "patch", split_axis=0, concat_axis=0, tiled=True)
    placed = jnp.dot(
        inbound, arrived.reshape(sources * capacity, -1), preferred_element_type=jnp.float32
    )
    slot_slips = placed.astype(jnp.bfloat16).reshape(slot_width, gathered.shape[1], samples)
    kernels = green_tiles[0]
    own_rows = slot_slips.shape[1] // sources
    result = lax.psum_scatter(
        convolve_rows(slot_slips, kernels, own_rows * lax.axis_size("patch")),
        "patch",
        scatter_dimension=0,
        tiled=True,
    )
    return result[None]


def solution(mesh):
    in_specs = (P("patch", "site", None), P("site", "patch", None, None), P())
    out_specs = P("site", "patch", None, None)
    return jax.shard_map(local, mesh=mesh, in_specs=in_specs, out_specs=out_specs, check_vma=False)
```

profile of v0, /device:TPU:1, one launch (start us, length us, event | category | flops | bytes accessed | tf_op | source)
XLA Modules:
  0.0 327.7 jit_solution(13415013174295641331)
XLA Ops:
  8.2 31.8 %all_gather.3 = bf16[16,64,256]{2,0,1:T(8,128)(2,1)S(1)} all-gather(bf16[16,4,256]{2,0,1:T(8,128)(2,1)S(1)} %copy.35), channel_id=1, replica_groups=mesh['site'=16,'patch'=32] {'site'}, dimensions={1}, use_global_device_ids=true | all-gather | bytes 557056 | tf_op jit(solution)/shard_map/all_gather | solution.py:91
  41.0 2.7 reshape.44
  43.6 15.3 %all-to-all-start = ((bf16[32,2,16384]{2,1,0:T(2,128)(2,1)}), bf16[32,2,16384]{2,1,0:T(2,128)(2,1)S(1)}, u32[]{:S(2)}, u32[]{:S(2)}) async-start(bf16[32,2,16384]{2,1,0:T(2,128)(2,1)} %reshape.44), calls=%async_computation | async-start | bytes 4194304 | tf_op jit(solution)/shard_map/all_to_all | solution.py:95
  59.2 28.1 %all-to-all-done = bf16[32,2,16384]{2,1,0:T(2,128)(2,1)S(1)} async-done(((bf16[32,2,16384]{2,1,0:T(2,128)(2,1)}), bf16[32,2,16384]{2,1,0:T(2,128)(2,1)S(1)}, u32[]{:S(2)}, u32[]{:S(2)}) %all-to-all-start) | async-done | bytes 2097184 | tf_op jit(solution)/shard_map/all_to_all | solution.py:95
  87.3 2.2 reshape.45
  89.5 2.3 convolution_convert_fusion.1
  91.8 100.3 %while.13 = (s32[]{:T(128)}, f32[64,2,1280]{2,0,1:T(8,128)S(1)}, bf16[4,8,64,256]{3,1,2,0:T(8,128)(2,1)S(1)}, bf16[4,8,2,1024]{3,2,1,0:T(2,128)(2,1)}, s32[]{:T(128)}, /*index=5*/bf16[]{:T(256)}, s32[]{:T(128)}) while((s32[]{:T(128)}, f32[64,2,1280]{2,0,1:T(8,128)S(1)}, bf16[4,8,64,256]{3,1,2,0:T(8,128)(2,1)S(1)}, ...), condition=%wide.region_2.3_spmd.clone, body=%wide.region_1.2_spmd.clone.sunk | while | flops 671580160 | bytes 46121056 | solution.py:51
  93.0 2.9 slice.68
  95.9 13.7 %reshape.54 = bf16[8,2,128,1535]{3,2,0,1:T(8,128)(2,1)} reshape(bf16[8,2,196480]{2,0,1:T(8,128)(2,1)} %slice.68) | data formatting | bytes 12574720 | tf_op jit(solution)/shard_map/while/body/eval_jaxpr/reshape | solution.py:16
  109.7 3.5 %fusion.36 = f32[64,2,1280]{2,0,1:T(8,128)S(1)} fusion(bf16[8,2,128,1535]{3,2,0,1:T(8,128)(2,1)} %reshape.54, bf16[8,64,256]{2,1,0:T(8,128)(2,1)S(1)} %bitcast.49), kind=kOutput, calls=%fused_computation.7.clone.1 | convolution fusion | flops 335544320 | bytes 6029312 | tf_op jit(solution)/shard_map/while/body/eval_jaxpr/pvq,pcqt->vct/dot_general | solution.py:43
  113.2 3.7 %fusion.37 = f32[64,2,1280]{2,0,1:T(8,128)S(1)} fusion(f32[64,2,1280]{2,0,1:T(8,128)S(1)} %fusion.36, bf16[8,2,128,1535]{3,2,0,1:T(8,128)(2,1)} %reshape.54, f32[64,2,1280]{2,0,1:T(8,128)S(1)} %get-tuple-element.141, pred[]{:T(512)S(6)} %compare.7, bf16[8,64,256]{2,1,0:T(8,128)(2,1)S(1)} %bitcast.50), kind=kOutput, calls=%fused_computation.6.clone.1 | convolution fusion | flops 336035840 | bytes 7340033 | tf_op jit(solution)/shard_map/while/body/eval_jaxpr/pvq,pcqt->vct/dot_general | solution.py:37
  118.1 2.9 slice.68
  121.0 13.7 %reshape.54 = bf16[8,2,128,1535]{3,2,0,1:T(8,128)(2,1)} reshape(bf16[8,2,196480]{2,0,1:T(8,128)(2,1)} %slice.68) | data formatting | bytes 12574720 | tf_op jit(solution)/shard_map/while/body/eval_jaxpr/reshape | solution.py:16
  134.8 3.5 %fusion.36 = f32[64,2,1280]{2,0,1:T(8,128)S(1)} fusion(bf16[8,2,128,1535]{3,2,0,1:T(8,128)(2,1)} %reshape.54, bf16[8,64,256]{2,1,0:T(8,128)(2,1)S(1)} %bitcast.49), kind=kOutput, calls=%fused_computation.7.clone.1 | convolution fusion | flops 335544320 | bytes 6029312 | tf_op jit(solution)/shard_map/while/body/eval_jaxpr/pvq,pcqt->vct/dot_general | solution.py:43
  138.3 3.7 %fusion.37 = f32[64,2,1280]{2,0,1:T(8,128)S(1)} fusion(f32[64,2,1280]{2,0,1:T(8,128)S(1)} %fusion.36, bf16[8,2,128,1535]{3,2,0,1:T(8,128)(2,1)} %reshape.54, f32[64,2,1280]{2,0,1:T(8,128)S(1)} %get-tuple-element.141, pred[]{:T(512)S(6)} %compare.7, bf16[8,64,256]{2,1,0:T(8,128)(2,1)S(1)} %bitcast.50), kind=kOutput, calls=%fused_computation.6.clone.1 | convolution fusion | flops 336035840 | bytes 7340033 | tf_op jit(solution)/shard_map/while/body/eval_jaxpr/pvq,pcqt->vct/dot_general | solution.py:37
  143.2 2.9 slice.68
  146.1 13.7 %reshape.54 = bf16[8,2,128,1535]{3,2,0,1:T(8,128)(2,1)} reshape(bf16[8,2,196480]{2,0,1:T(8,128)(2,1)} %slice.68) | data formatting | bytes 12574720 | tf_op jit(solution)/shard_map/while/body/eval_jaxpr/reshape | solution.py:16
  159.8 3.5 %fusion.36 = f32[64,2,1280]{2,0,1:T(8,128)S(1)} fusion(bf16[8,2,128,1535]{3,2,0,1:T(8,128)(2,1)} %reshape.54, bf16[8,64,256]{2,1,0:T(8,128)(2,1)S(1)} %bitcast.49), kind=kOutput, calls=%fused_computation.7.clone.1 | convolution fusion | flops 335544320 | bytes 6029312 | tf_op jit(solution)/shard_map/while/body/eval_jaxpr/pvq,pcqt->vct/dot_general | solution.py:43
  163.3 3.7 %fusion.37 = f32[64,2,1280]{2,0,1:T(8,128)S(1)} fusion(f32[64,2,1280]{2,0,1:T(8,128)S(1)} %fusion.36, bf16[8,2,128,1535]{3,2,0,1:T(8,128)(2,1)} %reshape.54, f32[64,2,1280]{2,0,1:T(8,128)S(1)} %get-tuple-element.141, pred[]{:T(512)S(6)} %compare.7, bf16[8,64,256]{2,1,0:T(8,128)(2,1)S(1)} %bitcast.50), kind=kOutput, calls=%fused_computation.6.clone.1 | convolution fusion | flops 336035840 | bytes 7340033 | tf_op jit(solution)/shard_map/while/body/eval_jaxpr/pvq,pcqt->vct/dot_general | solution.py:37
  168.3 2.9 slice.68
  171.2 13.7 %reshape.54 = bf16[8,2,128,1535]{3,2,0,1:T(8,128)(2,1)} reshape(bf16[8,2,196480]{2,0,1:T(8,128)(2,1)} %slice.68) | data formatting | bytes 12574720 | tf_op jit(solution)/shard_map/while/body/eval_jaxpr/reshape | solution.py:16
  184.9 3.5 %fusion.36 = f32[64,2,1280]{2,0,1:T(8,128)S(1)} fusion(bf16[8,2,128,1535]{3,2,0,1:T(8,128)(2,1)} %reshape.54, bf16[8,64,256]{2,1,0:T(8,128)(2,1)S(1)} %bitcast.49), kind=kOutput, calls=%fused_computation.7.clone.1 | convolution fusion | flops 335544320 | bytes 6029312 | tf_op jit(solution)/shard_map/while/body/eval_jaxpr/pvq,pcqt->vct/dot_general | solution.py:43
  188.4 3.7 %fusion.37 = f32[64,2,1280]{2,0,1:T(8,128)S(1)} fusion(f32[64,2,1280]{2,0,1:T(8,128)S(1)} %fusion.36, bf16[8,2,128,1535]{3,2,0,1:T(8,128)(2,1)} %reshape.54, f32[64,2,1280]{2,0,1:T(8,128)S(1)} %get-tuple-element.141, pred[]{:T(512)S(6)} %compare.7, bf16[8,64,256]{2,1,0:T(8,128)(2,1)S(1)} %bitcast.50), kind=kOutput, calls=%fused_computation.6.clone.1 | convolution fusion | flops 336035840 | bytes 7340033 | tf_op jit(solution)/shard_map/while/body/eval_jaxpr/pvq,pcqt->vct/dot_general | solution.py:37
  195.4 124.1 %all-reduce.4.cloned.1.call-done = f32[64,2,1280]{2,1,0:T(2,128)} async-done(((f32[64,2,1280]{2,1,0:T(2,128)}), f32[64,2,1280]{2,1,0:T(2,128)}) %all-reduce.4.cloned.1.call-update) | async-done | bytes 655376
  (46 shorter events, 11.9 us)
Async XLA Ops:
  40.3 18.9 %copy-start = (s32[512]{0:T(512)S(1)}, s32[512]{0:T(512)}, u32[]{:S(2)}) copy-start(s32[512]{0:T(512)} %param.7) | copy-start | bytes 6148
  43.6 43.7 %all-to-all-start = ((bf16[32,2,16384]{2,1,0:T(2,128)(2,1)}), bf16[32,2,16384]{2,1,0:T(2,128)(2,1)S(1)}, u32[]{:S(2)}, u32[]{:S(2)}) async-start(bf16[32,2,16384]{2,1,0:T(2,128)(2,1)} %reshape.44), calls=%async_computation | async-start | bytes 4194304 | tf_op jit(solution)/shard_map/all_to_all | solution.py:95
  59.0 260.6 %all-reduce.4.cloned.1.call-start = ((), (), s32[]{:S(2)}) async-start(), calls=%async_computation.1 | async-start | bytes 1310720
Sparse Core Ops, SparseCore 0:
  193.6 125.8 all-reduce.3
where the time goes:
time: 329 us; the launch traced here: 328 us
  waiting for transfers between devices  152 us (46%)
  local copies, waits for them, and re-layouts  81.3 us (25%)
  blocking collectives  31.8 us (10%)
  matrix products  31.6 us (10%)
  starting transfers between devices  15.4 us (5%)
  between operations  14.1 us (4%)
    unnamed x2, waiting for transfers between devices  124 us
    reshape x4, local copies, waits for them, and re-layouts, band_matrix(): repeated[..., :half_len * (period - 1)]  54.7 us
    all_gather x1, blocking collectives, local(): gathered = lax.all_gather(slip_rates, 'site', axis=1, tiled=True)  31.8 us
    all_to_all x1, waiting for transfers between devices, local(): lax.all_to_all(outgoing, 'patch', split_axis=0, concat_axis=0, tiled=True)  28.1 us
    all_to_all x1, starting transfers between devices, local(): lax.all_to_all(outgoing, 'patch', split_axis=0, concat_axis=0, tiled=True)  15.3 us
    dot_general x4, matrix products, accumulate(): jnp.einsum('pvq,pcqt->vct', slip_block[..., :half_len], band_rows[..., ha...  14.7 us
    dot_general x4, matrix products, accumulate(): jnp.einsum('pvq,pcqt->vct', slip_block[..., half_len:], band_rows[..., :l...  14 us
    slice x4, local copies, waits for them, and re-layouts, band_matrix(): repeated[..., :half_len * (period - 1)]  11.6 us
  transfers between devices with their start and end apart: 2, of which 2 were waited for; matrix products, arithmetic and copies ran while one was open for 0% of the time, Pallas kernels for 0%

commit v1 on v0

v1 whole, which is shorter than its diff:
```python
import functools

import jax
import jax.numpy as jnp
from jax import lax
from jax.experimental import pallas as pl
from jax.experimental.pallas import tpu as pltpu
from jax.sharding import PartitionSpec as P

MESH = pl.DeviceIdType.MESH
BLOCK = 32
LANES = 128


def right_slot(k, nz):
    return 2 * k - 1


def left_slot(k, nz):
    return 2 * k


def kernel(
    nz, npd, tab_out, tab_in, slip_ref, green_ref, out_ref,
    gath, outg, arrived, band, prod, part, recv,
    zsend, zrecv, gsend, grecv, rsend, rrecv,
):
    z = lax.axis_index("site")
    me = lax.axis_index("patch")
    patches = tab_in.shape[0]
    lags = green_ref.shape[2]
    tiles = lags // LANES
    width = lags + LANES
    out_len = out_ref.shape[2]
    rows = slip_ref.shape[0]

    barrier = pltpu.get_barrier_semaphore()
    for step in (2, nz - 2, 1, nz - 1):
        pl.semaphore_signal(
            barrier, inc=1, device_id=(lax.rem(z + step, nz), me), device_id_type=MESH
        )

    def greet(i, carry):
        pl.semaphore_signal(
            barrier, inc=1, device_id=(z, lax.rem(me + i, npd)), device_id_type=MESH
        )
        return carry

    lax.fori_loop(1, npd, greet, 0)

    for entry in range(2 * npd):
        outg[entry] = green_ref[tab_out[entry]]
    gath[0] = slip_ref[...]

    pl.semaphore_wait(barrier, npd - 1 + 4)

    def zcopy(direction, k):
        slot_of = right_slot if direction == 1 else left_slot
        hop = 1 if k % 2 else 2
        source = slip_ref if k == hop else gath.at[slot_of(k - hop, nz)]
        slot = slot_of(k, nz)
        target = lax.rem(z + (hop if direction == 1 else nz - hop), nz)
        return pltpu.make_async_remote_copy(
            src_ref=source,
            dst_ref=gath.at[slot],
            send_sem=zsend.at[slot],
            recv_sem=zrecv.at[slot],
            device_id=(target, me),
            device_id_type=MESH,
        )

    reach_right = nz // 2
    reach_left = nz - 1 - reach_right

    def relay(done):
        for k in (done + 2, done + 1):
            if k <= reach_right:
                zcopy(1, k).start()
            if k <= reach_left:
                zcopy(-1, k).start()

    def zwait(k):
        if k <= reach_right:
            zcopy(1, k).wait_recv()
        if k <= reach_left:
            zcopy(-1, k).wait_recv()

    relay(0)

    def gcopy(i):
        peer = lax.rem(me + i, npd)
        return pltpu.make_async_remote_copy(
            src_ref=outg.at[pl.ds(2 * peer, 2)],
            dst_ref=arrived.at[pl.ds(2 * me, 2)],
            send_sem=gsend.at[peer],
            recv_sem=grecv.at[me],
            device_id=(z, peer),
            device_id_type=MESH,
        )

    def gstart(i, carry):
        gcopy(i).start()
        return carry

    lax.fori_loop(1, npd, gstart, 0)
    keep = pltpu.make_async_copy(
        outg.at[pl.ds(2 * me, 2)], arrived.at[pl.ds(2 * me, 2)], grecv.at[me]
    )
    keep.start()

    zwait(2)
    relay(2)

    def gwait(i, carry):
        pltpu.make_async_copy(
            outg.at[pl.ds(2 * i, 2)], arrived.at[pl.ds(2 * i, 2)], grecv.at[i]
        ).wait()
        return carry

    lax.fori_loop(0, npd, gwait, 0)
    zwait(4)
    relay(4)

    row_of = lax.broadcasted_iota(jnp.int32, (BLOCK, LANES), 0)
    lane_of = lax.broadcasted_iota(jnp.int32, (BLOCK, LANES), 1)
    inside = lane_of >= row_of

    def build(p, carry):
        tile = arrived[tab_in[p]].astype(jnp.float32)
        at = pl.multiple_of(p * BLOCK, BLOCK)
        for c in range(2):
            before = jnp.zeros((BLOCK, LANES), jnp.float32)
            for m in range(tiles + 1):
                if m < tiles:
                    row = tile[c : c + 1, m * LANES : (m + 1) * LANES]
                    turned = pltpu.roll(
                        jnp.broadcast_to(row, (BLOCK, LANES)), 0, 1, stride=1, stride_axis=0
                    )
                else:
                    turned = jnp.zeros((BLOCK, LANES), jnp.float32)
                block = jnp.where(inside, turned, before)
                before = turned
                start = c * width + m * LANES
                band[pl.ds(at, BLOCK), start : start + LANES] = block.astype(jnp.bfloat16)
        return carry

    lax.fori_loop(0, patches, build, 0)

    sub = lax.broadcasted_iota(jnp.int32, (8, out_len), 0)
    pad = jnp.zeros((8, LANES), jnp.float32)

    def rcopy(slot, h, chip):
        target = 2 * chip + h
        return target, pltpu.make_async_remote_copy(
            src_ref=part.at[2 * slot + h],
            dst_ref=recv.at[me],
            send_sem=rsend.at[2 * slot + h],
            recv_sem=rrecv.at[me],
            device_id=(z, target),
            device_id_type=MESH,
        )

    def chip_of(slot):
        if slot == 0:
            return z
        k = (slot + 1) // 2
        return lax.rem(z + (nz - k if slot % 2 else k), nz)

    def compute(first, last):
        count = last - first
        left = gath[first:last].reshape(count * rows, gath.shape[2])
        step = 256
        for n in range(0, 2 * width, step):
            prod[0 : count * rows, n : n + step] = jnp.dot(
                left, band[:, n : n + step], preferred_element_type=jnp.float32
            )
        for slot in range(first, last):
            base = (slot - first) * rows
            sums, turned = [], []
            for c in range(2):
                u = [
                    prod[base + 8 * i : base + 8 * i + 8, c * width : (c + 1) * width]
                    for i in range(4)
                ]
                even = jnp.concatenate([u[0], pad], 1) + jnp.concatenate([pad, u[2]], 1)
                odd = jnp.concatenate([u[1], pad], 1) + jnp.concatenate([pad, u[3]], 1)
                total = even + pltpu.roll(odd, 2 * BLOCK, 1)
                sums.append(total)
                turned.append(pltpu.roll(total, BLOCK, 1))
            result = jnp.where(sub < 4, sums[0], pltpu.roll(sums[1], 4, 0)) + jnp.where(
                sub < 4, pltpu.roll(turned[0], 4, 0), turned[1]
            )
            for h in range(2):
                part[2 * slot + h, 0:2] = result[2 * h : 2 * h + 2]
                part[2 * slot + h, 2:4] = result[4 + 2 * h : 6 + 2 * h]
            chip = chip_of(slot)
            for h in range(2):
                target, copy = rcopy(slot, h, chip)

                @pl.when(target != me)
                def _():
                    copy.start()

                @pl.when(target == me)
                def _():
                    pltpu.make_async_copy(
                        part.at[2 * slot + h], recv.at[me], rrecv.at[me]
                    ).start()

    zwait(1)
    compute(0, 5)
    zwait(6)
    relay(6)
    zwait(3)
    compute(5, 9)
    zwait(5)
    compute(9, 13)
    zwait(7)
    zwait(8)
    compute(13, 16)

    def rwait(i, carry):
        pltpu.make_async_copy(part.at[i], recv.at[i], rrecv.at[i]).wait()
        return carry

    lax.fori_loop(0, npd, rwait, 0)
    total = jnp.sum(recv[...], axis=0)
    for v in range(2):
        for c in range(2):
            out_ref[v, c : c + 1] = total[2 * c + v : 2 * c + v + 1]

    for k in range(1, reach_right + 1):
        zcopy(1, k).wait_send()
    for k in range(1, reach_left + 1):
        zcopy(-1, k).wait_send()

    def gdrain(i, carry):
        gcopy(i).wait_send()
        return carry

    lax.fori_loop(1, npd, gdrain, 0)
    for slot in range(nz):
        chip = chip_of(slot)
        for h in range(2):
            target, copy = rcopy(slot, h, chip)

            @pl.when(target != me)
            def _():
                copy.wait_send()


def route_tables(patch_slot, slot_width, devices, me):
    owners = (patch_slot // slot_width).reshape(devices, -1)
    within = (patch_slot % slot_width).reshape(devices, -1)
    count = owners.shape[1]
    earlier = lax.broadcasted_iota(jnp.int32, (count, count), 1) < lax.broadcasted_iota(
        jnp.int32, (count, count), 0
    )
    same = owners[:, :, None] == owners[:, None, :]
    rank = jnp.sum((same & earlier[None]).astype(jnp.int32), axis=2)
    ranks = lax.broadcasted_iota(jnp.int32, (1, 2, 1), 1)
    mine = (owners[:, None, :] == me) & (rank[:, None, :] == ranks)
    tab_out = jnp.sum(jnp.where(mine, within[:, None, :], 0), axis=2).reshape(-1)
    source = lax.broadcasted_iota(jnp.int32, owners.shape, 0)
    tab_in = jnp.sum(jnp.where(source == me, owners * 2 + rank, 0), axis=0)
    return tab_out, tab_in


def local(nz, npd, slip_rates, green_tiles, patch_slot):
    me = lax.axis_index("patch")
    patches, own_v, samples = slip_rates.shape
    slot_width, lags = green_tiles.shape[1], green_tiles.shape[3]
    blocks = samples // BLOCK
    assert own_v == 4 and blocks == 8 and npd == 2 * nz and nz == 16
    tab_out, tab_in = route_tables(patch_slot, slot_width, npd, me)
    rows, depth = blocks * own_v, patches * BLOCK
    chunk = (
        slip_rates.reshape(patches, own_v, blocks, BLOCK).transpose(2, 1, 0, 3).reshape(rows, depth)
    )
    width, out_len = lags + LANES, lags + samples
    vmem = pl.BlockSpec(memory_space=pltpu.VMEM)
    smem = pl.BlockSpec(memory_space=pltpu.SMEM)
    dma = pltpu.SemaphoreType.DMA
    result = pl.pallas_call(
        functools.partial(kernel, nz, npd),
        out_shape=jax.ShapeDtypeStruct((2, 2, out_len), jnp.float32),
        in_specs=[smem, smem, vmem, vmem],
        out_specs=vmem,
        scratch_shapes=[
            pltpu.VMEM((nz, rows, depth), jnp.bfloat16),
            pltpu.VMEM((2 * npd, 2, lags), jnp.bfloat16),
            pltpu.VMEM((2 * npd, 2, lags), jnp.bfloat16),
            pltpu.VMEM((depth, 2 * width), jnp.bfloat16),
            pltpu.VMEM((5 * rows, 2 * width), jnp.float32),
            pltpu.VMEM((2 * nz, 4, out_len), jnp.float32),
            pltpu.VMEM((npd, 4, out_len), jnp.float32),
            dma((nz,)), dma((nz,)), dma((npd,)), dma((npd,)), dma((2 * nz,)), dma((npd,)),
        ],
        compiler_params=pltpu.CompilerParams(collective_id=0, has_side_effects=True),
    )(tab_out, tab_in, chunk, green_tiles[0])
    return result[None]


def solution(mesh):
    in_specs = (P("patch", "site", None), P("site", "patch", None, None), P())
    out_specs = P("site", "patch", None, None)
    return jax.shard_map(
        functools.partial(local, mesh.shape["site"], mesh.shape["patch"]),
        mesh=mesh, in_specs=in_specs, out_specs=out_specs, check_vma=False,
    )
```

time: 329 us -> 46.6 us (0.14)
  the two profiles are of different devices: /device:TPU:1 before, /device:TPU:4 now
where the time goes in v1:
time: 46.6 us; the launch traced here: 46 us
  Pallas kernels  41.1 us (88%)
  local copies, waits for them, and re-layouts  4.04 us (9%)
  other arithmetic  0.84 us (2%)
    pallas_call x1, Pallas kernels, local(): pl.pallas_call(functools.partial(kernel, nz, npd), out_shape=jax.ShapeDty...  41.1 us
    unnamed x5, local copies, waits for them, and re-layouts  2.02 us

profile of v1, /device:TPU:4, one launch (start us, length us, event | category | flops | bytes accessed | tf_op | source)
XLA Modules:
  0.0 46.0 jit_solution(10366211187825938091)
XLA Ops:
  0.0 0.0 copy-start.1
  0.0 0.7 %copy-done.1 = s32[512]{0:T(512)S(1)} copy-done((s32[512]{0:T(512)S(1)}, s32[512]{0:T(512)}, u32[]{:S(2)}) %copy-start.1) | copy-done | bytes 2072
  0.7 0.1 broadcast_in_dim_reshape.2
  0.8 0.1 copy.7
  0.9 0.1 copy.6
  0.9 0.1 convert_reduce_fusion
  1.1 0.7 %select_reduce_fusion.1.tab_in = s32[16]{0:T(128)} fusion(s32[32,16]{0,1:T(8,128)S(1)} %convert_reduce_fusion, s32[32,16]{0,1:T(8,128)S(1)} %copy.7, pred[32]{0:T(512)(128)(4,1)S(1)} %iota_compare_fusion.2), kind=kLoop, calls=%fused_computation.5 | loop fusion | flops 2032 | bytes 4192 | tf_op jit(solution)/shard_map/reduce_sum | solution.py:265
  1.7 0.1 broadcast_in_dim.23
  1.8 0.1 copy.9
  1.9 0.0 copy-start
  1.9 0.1 copy.10
  2.0 0.6 %reshape.28.tab_out = s32[64]{0:T(128)} reshape(s32[32,2]{1,0:T(8,128)S(1)} %copy.10) | data formatting | bytes 512 | tf_op jit(solution)/shard_map/reshape | solution.py:263
  2.6 0.0 copy-done
  2.6 0.1 reshape.29
  2.8 0.1 copy.14
  2.8 0.8 %reshape.30.slip_ref = bf16[32,512]{1,0:T(8,128)(2,1)} reshape(bf16[8,4,16,32]{3,2,1,0:T(8,128)(2,1)S(1)} %bitcast.7) | data formatting | bytes 65536 | tf_op jit(solution)/shard_map/reshape | solution.py:278
  3.6 41.1 %shard_map.37 = f32[2,2,1280]{2,1,0:T(2,128)} custom-call(s32[64]{0:T(128)} %reshape.28.tab_out, s32[16]{0:T(128)} %select_reduce_fusion.1.tab_in, bf16[32,512]{1,0:T(8,128)(2,1)} %reshape.30.slip_ref, bf16[32,2,1024]{2,1,0:T(2,128)(2,1)} %bitcast.8), custom_call_target="tpu_custom_call" | custom-call | tf_op jit(solution)/shard_map/pallas_call | solution.py:284
  44.7 1.3 %copy.16 = f32[1,2,2,1280]{3,2,1,0:T(2,128)} copy(f32[1,2,2,1280]{3,2,1,0:T(2,128)} %bitcast.9) | data formatting | bytes 40960
  (5 shorter events, 0.1 us)
Async XLA Ops:
  0.0 0.7 %copy-start.1 = (s32[512]{0:T(512)S(1)}, s32[512]{0:T(512)}, u32[]{:S(2)}) copy-start(s32[512]{0:T(512)} %param.5) | copy-start | bytes 6148
  1.9 0.8 %copy-start = (bf16[16,4,256]{2,1,0:T(4,128)(2,1)S(1)}, bf16[16,4,256]{2,1,0:T(4,128)(2,1)}, u32[]{:S(2)}) copy-start(bf16[16,4,256]{2,1,0:T(4,128)(2,1)} %param.3) | copy-start | bytes 98308

commit v2 on v1

v2 whole, which is shorter than its diff:
```python
import functools

import jax
import jax.numpy as jnp
from jax import lax
from jax.experimental import pallas as pl
from jax.experimental.pallas import tpu as pltpu
from jax.sharding import PartitionSpec as P

MESH = pl.DeviceIdType.MESH
BLOCK = 32
LANES = 128


ARRIVAL = (1, 3, 2, 4, 6, 5, 7, 8)
EAGER = 16


def z_slot(direction, k):
    return 1 + 2 * ARRIVAL.index(k) + (direction < 0)


def z_hop(k):
    return 2 if k == 8 else (3, 1, 1)[k % 3]


def kernel(
    nz, npd, slots_hbm, slip_ref, green_hbm, out_ref,
    slots, green_ref, gath, outg, arrived, band, prod, part, pair, recv,
    lsem, zsend, zrecv, gsend, grecv, psend, precv, rsend, rrecv,
):
    z = lax.axis_index("site")
    me = lax.axis_index("patch")
    side = 4
    chip_x, chip_y, core = me // (2 * side), lax.rem(me // 2, side), lax.rem(me, 2)
    my_chip = me // 2
    partner = me + 1 - 2 * core
    patches = slots.shape[0] // npd
    slot_width = green_ref.shape[0]
    lags = green_ref.shape[2]
    tiles = lags // LANES
    width = lags + LANES
    out_len = out_ref.shape[2]
    rows = slip_ref.shape[0]

    load_slots = pltpu.make_async_copy(slots_hbm, slots, lsem.at[0])
    load_green = pltpu.make_async_copy(green_hbm, green_ref, lsem.at[1])
    load_slots.start()
    load_green.start()

    def distance(offset):
        dx, dy, _ = offset
        return min(dx, side - dx) + min(dy, side - dy)

    offsets = [
        (dx, dy, other)
        for dx in range(side) for dy in range(side) for other in range(2)
    ]
    offsets = sorted(offsets, key=distance, reverse=True)[:-2] + [(0, 0, 1)]

    def peer_at(offset):
        dx, dy, other = offset
        chip = lax.rem(chip_x + dx, side) * side + lax.rem(chip_y + dy, side)
        return 2 * chip + (1 - core if other else core)

    barrier = pltpu.get_barrier_semaphore()
    z_steps = (3, nz - 3, 2, nz - 2, 1, nz - 1)
    for step in z_steps:
        pl.semaphore_signal(
            barrier, inc=1, device_id=(lax.rem(z + step, nz), me), device_id_type=MESH
        )
    for offset in offsets:
        pl.semaphore_signal(
            barrier, inc=1, device_id=(z, peer_at(offset)), device_id_type=MESH
        )

    load_slots.wait()
    load_green.wait()

    def pick(device, carry):
        first, last = jnp.int32(0), jnp.int32(0)
        values = [slots[device * patches + i] for i in range(patches)]
        hits = [value // slot_width == me for value in values]
        for i in range(patches):
            last = jnp.where(hits[i], values[i], last)
            j = patches - 1 - i
            first = jnp.where(hits[j], values[j], first)
        outg[2 * device] = green_ref[first % slot_width]
        outg[2 * device + 1] = green_ref[last % slot_width]
        return carry

    lax.fori_loop(0, npd, pick, 0)
    gath[0] = slip_ref[...]

    pl.semaphore_wait(barrier, npd - 1 + len(z_steps))

    def zcopy(direction, k):
        hop = z_hop(k)
        source = slip_ref if k == hop else gath.at[z_slot(direction, k - hop)]
        slot = z_slot(direction, k)
        target = lax.rem(z + (hop if direction == 1 else nz - hop), nz)
        return pltpu.make_async_remote_copy(
            src_ref=source,
            dst_ref=gath.at[slot],
            send_sem=zsend.at[slot],
            recv_sem=zrecv.at[slot],
            device_id=(target, me),
            device_id_type=MESH,
        )

    reach = {1: nz // 2, -1: nz - 1 - nz // 2}

    def zgo(k):
        for direction in (1, -1):
            if k <= reach[direction]:
                zcopy(direction, k).start()

    def zwait(k):
        for direction in (1, -1):
            if k <= reach[direction]:
                zcopy(direction, k).wait_recv()

    zgo(3)
    zgo(1)

    def gcopy(peer):
        return pltpu.make_async_remote_copy(
            src_ref=outg.at[pl.ds(2 * peer, 2)],
            dst_ref=arrived.at[pl.ds(2 * me, 2)],
            send_sem=gsend.at[peer],
            recv_sem=grecv.at[me],
            device_id=(z, peer),
            device_id_type=MESH,
        )

    for offset in offsets:
        gcopy(peer_at(offset)).start()
    keep = pltpu.make_async_copy(
        outg.at[pl.ds(2 * me, 2)], arrived.at[pl.ds(2 * me, 2)], grecv.at[me]
    )
    keep.start()

    def gwait(i, carry):
        pltpu.make_async_copy(
            outg.at[pl.ds(2 * i, 2)], arrived.at[pl.ds(2 * i, 2)], grecv.at[i]
        ).wait()
        return carry

    row_of = lax.broadcasted_iota(jnp.int32, (BLOCK, LANES), 0)
    lane_of = lax.broadcasted_iota(jnp.int32, (BLOCK, LANES), 1)
    inside = lane_of >= row_of

    def build(p, carry):
        owner = slots[me * patches + p] // slot_width
        rank = jnp.int32(0)
        for i in range(patches):
            same = slots[me * patches + i] // slot_width == owner
            rank = jnp.where(same & (p > i), 1, rank)
        tile = arrived[2 * owner + rank].astype(jnp.float32)
        at = pl.multiple_of(p * BLOCK, BLOCK)
        for c in range(2):
            before = jnp.zeros((BLOCK, LANES), jnp.float32)
            for m in range(tiles + 1):
                if m < tiles:
                    row = tile[c : c + 1, m * LANES : (m + 1) * LANES]
                    turned = pltpu.roll(
                        jnp.broadcast_to(row, (BLOCK, LANES)), 0, 1, stride=1, stride_axis=0
                    )
                else:
                    turned = jnp.zeros((BLOCK, LANES), jnp.float32)
                block = jnp.where(inside, turned, before)
                before = turned
                start = c * width + m * LANES
                band[pl.ds(at, BLOCK), start : start + LANES] = block.astype(jnp.bfloat16)
        return carry

    def prepare():
        lax.fori_loop(0, npd, gwait, 0)
        lax.fori_loop(0, patches, build, 0)

    eager = z < EAGER
    zwait(1)
    zgo(2)
    zwait(3)
    zgo(6)
    zgo(4)
    pl.when(eager)(prepare)
    zwait(4)
    zgo(5)
    zwait(6)
    zgo(8)
    zgo(7)
    pl.when(jnp.logical_not(eager))(prepare)

    sub = lax.broadcasted_iota(jnp.int32, (8, out_len), 0)
    pad = jnp.zeros((8, LANES), jnp.float32)

    def pcopy(slot):
        return pltpu.make_async_remote_copy(
            src_ref=part.at[2 * slot + 1 - core],
            dst_ref=pair.at[slot],
            send_sem=psend.at[slot],
            recv_sem=precv.at[slot],
            device_id=(z, partner),
            device_id_type=MESH,
        )

    def rcopy(slot):
        chip = chip_of(slot)
        return chip, pltpu.make_async_remote_copy(
            src_ref=part.at[2 * slot + core],
            dst_ref=recv.at[my_chip],
            send_sem=rsend.at[slot],
            recv_sem=rrecv.at[my_chip],
            device_id=(z, 2 * chip + core),
            device_id_type=MESH,
        )

    def chip_of(slot):
        if slot == 0:
            return z
        k = ARRIVAL[(slot - 1) // 2]
        return lax.rem(z + (nz - k if slot % 2 else k), nz)

    def compute(first, last):
        count = last - first
        left = gath[first:last].reshape(count * rows, gath.shape[2])
        step = 256
        for n in range(0, 2 * width, step):
            prod[0 : count * rows, n : n + step] = jnp.dot(
                left, band[:, n : n + step], preferred_element_type=jnp.float32
            )
        for slot in range(first, last):
            base = (slot - first) * rows
            sums, turned = [], []
            for c in range(2):
                u = [
                    prod[base + 8 * i : base + 8 * i + 8, c * width : (c + 1) * width]
                    for i in range(4)
                ]
                even = jnp.concatenate([u[0], pad], 1) + jnp.concatenate([pad, u[2]], 1)
                odd = jnp.concatenate([u[1], pad], 1) + jnp.concatenate([pad, u[3]], 1)
                total = even + pltpu.roll(odd, 2 * BLOCK, 1)
                sums.append(total)
                turned.append(pltpu.roll(total, BLOCK, 1))
            result = jnp.where(sub < 4, sums[0], pltpu.roll(sums[1], 4, 0)) + jnp.where(
                sub < 4, pltpu.roll(turned[0], 4, 0), turned[1]
            )
            for h in range(2):
                part[2 * slot + h, 0:2] = result[2 * h : 2 * h + 2]
                part[2 * slot + h, 2:4] = result[4 + 2 * h : 6 + 2 * h]
            pcopy(slot).start()

    def forward(first, last):
        for slot in range(first, last):
            pcopy(slot).wait_recv()
            part[2 * slot + core] = part[2 * slot + core] + pair[slot]
            chip, copy = rcopy(slot)

            @pl.when(chip != my_chip)
            def _():
                copy.start()

            @pl.when(chip == my_chip)
            def _():
                pltpu.make_async_copy(
                    part.at[2 * slot + core], recv.at[my_chip], rrecv.at[my_chip]
                ).start()

    zwait(2)
    compute(0, 7)
    zwait(5)
    compute(7, 13)
    forward(0, 7)
    pl.when(eager)(lambda: forward(7, 13))
    zwait(7)
    zwait(8)
    compute(13, 16)
    pl.when(jnp.logical_not(eager))(lambda: forward(7, 13))
    forward(13, 16)

    def rwait(i, carry):
        pltpu.make_async_copy(part.at[i], recv.at[i], rrecv.at[i]).wait()
        return carry

    lax.fori_loop(0, nz, rwait, 0)
    total = jnp.sum(recv[...], axis=0)
    for v in range(2):
        for c in range(2):
            out_ref[v, c : c + 1] = total[2 * c + v : 2 * c + v + 1]

    for direction in (1, -1):
        for k in range(1, reach[direction] + 1):
            zcopy(direction, k).wait_send()

    def gdrain(i, carry):
        @pl.when(i != me)
        def _():
            gcopy(i).wait_send()

        return carry

    lax.fori_loop(0, npd, gdrain, 0)
    for slot in range(nz):
        pcopy(slot).wait_send()
        chip, copy = rcopy(slot)

        @pl.when(chip != my_chip)
        def _():
            copy.wait_send()


def local(nz, npd, slip_rates, green_tiles, patch_slot):
    patches, own_v, samples = slip_rates.shape
    lags = green_tiles.shape[3]
    blocks = samples // BLOCK
    assert own_v == 4 and blocks == 8 and npd == 2 * nz and nz == 16
    rows, depth = blocks * own_v, patches * BLOCK
    chunk = (
        slip_rates.reshape(patches, own_v, blocks, BLOCK).transpose(2, 1, 0, 3).reshape(rows, depth)
    )
    width, out_len = lags + LANES, lags + samples
    vmem = pl.BlockSpec(memory_space=pltpu.VMEM)
    hbm = pl.BlockSpec(memory_space=pltpu.HBM)
    dma = pltpu.SemaphoreType.DMA
    result = pl.pallas_call(
        functools.partial(kernel, nz, npd),
        out_shape=jax.ShapeDtypeStruct((2, 2, out_len), jnp.float32),
        in_specs=[hbm, vmem, hbm],
        out_specs=vmem,
        scratch_shapes=[
            pltpu.SMEM(patch_slot.shape, jnp.int32),
            pltpu.VMEM(green_tiles.shape[1:], jnp.bfloat16),
            pltpu.VMEM((nz, rows, depth), jnp.bfloat16),
            pltpu.VMEM((2 * npd, 2, lags), jnp.bfloat16),
            pltpu.VMEM((2 * npd, 2, lags), jnp.bfloat16),
            pltpu.VMEM((depth, 2 * width), jnp.bfloat16),
            pltpu.VMEM((7 * rows, 2 * width), jnp.float32),
            pltpu.VMEM((2 * nz, 4, out_len), jnp.float32),
            pltpu.VMEM((nz, 4, out_len), jnp.float32),
            pltpu.VMEM((nz, 4, out_len), jnp.float32),
            dma((2,)), dma((nz,)), dma((nz,)), dma((npd,)), dma((npd,)),
            dma((nz,)), dma((nz,)), dma((nz,)), dma((nz,)),
        ],
        compiler_params=pltpu.CompilerParams(
            collective_id=0, has_side_effects=True, vmem_limit_bytes=16 * 1024 * 1024
        ),
    )(patch_slot, chunk, green_tiles[0])
    return result[None]


def solution(mesh):
    in_specs = (P("patch", "site", None), P("site", "patch", None, None), P())
    out_specs = P("site", "patch", None, None)
    return jax.shard_map(
        functools.partial(local, mesh.shape["site"], mesh.shape["patch"]),
        mesh=mesh, in_specs=in_specs, out_specs=out_specs, check_vma=False,
    )
```

time: 46.6 us -> 41.9 us (0.90)
  Pallas kernels: 41.1 us -> 39.3 us
  local copies, waits for them, and re-layouts: 4.04 us -> 2.45 us
  other arithmetic: 0.84 us -> 0 us
    pallas_call x1, Pallas kernels: 41.1 us -> 39.3 us  [local(): pl.pallas_call(functools.partial(kernel, nz, npd), out_shape=jax.ShapeDty...]
    reduce_sum x3 -> x0, other arithmetic: 0.81 us -> none  [the longest x1 0.66 us: route_tables(): tab_in = jnp.sum(jnp.where(source == me, owners * 2 + rank, 0), axis=0)]
    unnamed x5, local copies, waits for them, and re-layouts: 2.02 us -> 1.35 us
    reshape x1 -> x0, local copies, waits for them, and re-layouts: 0.62 us -> none  [route_tables(): jnp.sum(jnp.where(mine, within[:, None, :], 0), axis=2).reshape(-1)]
where the time goes in v2:
time: 41.9 us; the launch traced here: 41.7 us
  Pallas kernels  39.3 us (94%)
  local copies, waits for them, and re-layouts  2.45 us (6%)
    pallas_call x1, Pallas kernels, local(): pl.pallas_call(functools.partial(kernel, nz, npd), out_shape=jax.ShapeDty...  39.3 us
    unnamed x5, local copies, waits for them, and re-layouts  1.35 us
    reshape x3, local copies, waits for them, and re-layouts, local(): slip_rates.reshape(patches, own_v, blocks, BLOCK).transpose(2, 1, 0, 3)  1.1 us

profile of v2, /device:TPU:4, one launch (start us, length us, event | category | flops | bytes accessed | tf_op | source)
XLA Modules:
  0.0 41.7 jit_solution(10697387485581585076)
XLA Ops:
  0.0 0.9 %reshape.6 = bf16[16,4,8,32]{3,2,1,0:T(8,128)(2,1)S(1)} reshape(bf16[16,4,256]{2,1,0:T(4,128)(2,1)} %param.3) | data formatting | bytes 65536 | tf_op jit(solution)/shard_map/reshape | solution.py:320
  0.9 0.1 copy.6
  1.0 0.0 copy-start
  1.0 0.0 copy-start.1
  1.0 0.2 reshape.7.slip_ref
  1.1 0.7 %copy-done = bf16[1,32,2,1024]{3,2,1,0:T(2,128)(2,1)S(1)} copy-done((bf16[1,32,2,1024]{3,2,1,0:T(2,128)(2,1)S(1)}, bf16[1,32,2,1024]{3,2,1,0:T(2,128)(2,1)}, u32[]{:S(2)}) %copy-start) | copy-done | bytes 131096
  1.9 0.0 copy-done.1
  1.9 39.3 %shard_map.37 = f32[2,2,1280]{2,1,0:T(2,128)S(1)} custom-call(s32[512]{0:T(512)S(1)} %copy-done.1, bf16[32,512]{1,0:T(8,128)(2,1)S(1)} %reshape.7.slip_ref, bf16[32,2,1024]{2,1,0:T(2,128)(2,1)S(1)} %bitcast.7), custom_call_target="tpu_custom_call" | custom-call | tf_op jit(solution)/shard_map/pallas_call | solution.py:326
  41.1 0.6 %copy.8 = f32[1,2,2,1280]{3,2,1,0:T(2,128)} copy(f32[1,2,2,1280]{3,2,1,0:T(2,128)S(1)} %bitcast.8) | data formatting | bytes 40960
Async XLA Ops:
  1.0 0.9 %copy-start = (bf16[1,32,2,1024]{3,2,1,0:T(2,128)(2,1)S(1)}, bf16[1,32,2,1024]{3,2,1,0:T(2,128)(2,1)}, u32[]{:S(2)}) copy-start(bf16[1,32,2,1024]{3,2,1,0:T(2,128)(2,1)} %param.4) | copy-start | bytes 393220
  1.0 0.9 %copy-start.1 = (s32[512]{0:T(512)S(1)}, s32[512]{0:T(512)}, u32[]{:S(2)}) copy-start(s32[512]{0:T(512)} %slots_hbm.1) | copy-start | bytes 6148

commit v3 on v2

v3 whole, which is shorter than its diff:
```python
import functools

import jax
import jax.numpy as jnp
from jax import lax
from jax.experimental import pallas as pl
from jax.experimental.pallas import tpu as pltpu
from jax.sharding import PartitionSpec as P

MESH = pl.DeviceIdType.MESH
BLOCK = 32
LANES = 128


ARRIVAL = (1, 3, 2, 4, 6, 5, 7, 8)


def z_slot(direction, k):
    return 1 + 2 * ARRIVAL.index(k) + (direction < 0)


def z_hop(k):
    return 2 if k == 8 else (3, 1, 1)[k % 3]


def kernel(
    nz, npd, slots_hbm, slip_ref, green_hbm, out_ref,
    slots, places, green_ref, gath, outg, arrived, tiles_ref, band, prod, part, recv,
    lsem, zsend, zrecv, gsend, grecv, psend, precv, rsend, rrecv,
):
    z = lax.axis_index("site")
    me = lax.axis_index("patch")
    side = 4
    chip_x, chip_y, core = me // (2 * side), lax.rem(me // 2, side), lax.rem(me, 2)
    my_chip = me // 2
    partner = me + 1 - 2 * core
    patches = slots.shape[0] // npd
    slot_width = green_ref.shape[0]
    lags = green_ref.shape[2]
    tiles = lags // LANES
    width = lags + LANES
    out_len = out_ref.shape[2]
    rows, depth = slip_ref.shape[1:]

    load_slots = pltpu.make_async_copy(slots_hbm, slots, lsem.at[0])
    load_green = pltpu.make_async_copy(green_hbm, green_ref, lsem.at[1])
    load_slots.start()
    load_green.start()

    def distance(offset):
        dx, dy, _ = offset
        return min(dx, side - dx) + min(dy, side - dy)

    offsets = [
        (dx, dy, other)
        for dx in range(side) for dy in range(side) for other in range(2)
    ]
    offsets = sorted(offsets, key=distance, reverse=True)[:-2] + [(0, 0, 1)]

    def peer_at(offset):
        dx, dy, other = offset
        chip = lax.rem(chip_x + dx, side) * side + lax.rem(chip_y + dy, side)
        return 2 * chip + (1 - core if other else core)

    barrier = pltpu.get_barrier_semaphore()
    greetings = 0
    for step in (3, nz - 3, 2, nz - 2, 1, nz - 1):
        for receiver in (me, partner) if step in (3, nz - 3, 1, nz - 1) else (me,):
            pl.semaphore_signal(
                barrier, inc=1, device_id=(lax.rem(z + step, nz), receiver), device_id_type=MESH
            )
            greetings += 1
    for offset in offsets:
        pl.semaphore_signal(
            barrier, inc=1, device_id=(z, peer_at(offset)), device_id_type=MESH
        )

    load_slots.wait()
    load_green.wait()

    def pick(device, carry):
        first, last = jnp.int32(0), jnp.int32(0)
        values = [slots[device * patches + i] for i in range(patches)]
        hits = [value // slot_width == me for value in values]
        for i in range(patches):
            last = jnp.where(hits[i], values[i], last)
            j = patches - 1 - i
            first = jnp.where(hits[j], values[j], first)
        outg[2 * device] = green_ref[first % slot_width]
        outg[2 * device + 1] = green_ref[last % slot_width]
        return carry

    lax.fori_loop(0, npd, pick, 0)

    owners = [slots[me * patches + i] // slot_width for i in range(patches)]
    for i in range(patches):
        rank = jnp.int32(0)
        for j in range(i):
            rank = jnp.where(owners[j] == owners[i], 1, rank)
        places[i] = 2 * owners[i] + rank

    pl.semaphore_wait(barrier, npd - 1 + greetings)

    def half_of(slot, half):
        return gath.at[slot, :, half * depth : (half + 1) * depth]

    swap = pltpu.make_async_remote_copy(
        src_ref=slip_ref.at[1 - core],
        dst_ref=half_of(0, 1),
        send_sem=zsend.at[0, 1],
        recv_sem=zrecv.at[0, 1],
        device_id=(z, partner),
        device_id_type=MESH,
    )
    def zcopy(direction, k, half):
        hop = z_hop(k)
        slot = z_slot(direction, k)
        target, receiver = lax.rem(z + (hop if direction == 1 else nz - hop), nz), me
        if k > hop:
            source = half_of(z_slot(direction, k - hop), half)
        elif half:
            source, receiver = slip_ref.at[1 - core], partner
        else:
            source = slip_ref.at[core]
        return pltpu.make_async_remote_copy(
            src_ref=source,
            dst_ref=half_of(slot, half),
            send_sem=zsend.at[slot, half],
            recv_sem=zrecv.at[slot, half],
            device_id=(target, receiver),
            device_id_type=MESH,
        )

    reach = {1: nz // 2, -1: nz - 1 - nz // 2}

    def zgo(k, half):
        for direction in (1, -1):
            if k <= reach[direction]:
                zcopy(direction, k, half).start()

    def zwait(k, half):
        for direction in (1, -1):
            if k <= reach[direction]:
                zcopy(direction, k, half).wait_recv()

    def zrelay(k, after):
        for half in range(2):
            zwait(k, half)
            for onward in after:
                zgo(onward, half)

    for k in (3, 1):
        for half in range(2):
            zgo(k, half)
    swap.start()
    gath[0, :, 0:depth] = slip_ref[core]

    def gcopy(peer):
        return pltpu.make_async_remote_copy(
            src_ref=outg.at[pl.ds(2 * peer, 2)],
            dst_ref=arrived.at[pl.ds(2 * me, 2)],
            send_sem=gsend.at[peer],
            recv_sem=grecv.at[me],
            device_id=(z, peer),
            device_id_type=MESH,
        )

    for offset in offsets:
        gcopy(peer_at(offset)).start()
    keep = pltpu.make_async_copy(
        outg.at[pl.ds(2 * me, 2)], arrived.at[pl.ds(2 * me, 2)], grecv.at[me]
    )
    keep.start()

    def gwait(i, carry):
        pltpu.make_async_copy(
            outg.at[pl.ds(2 * i, 2)], arrived.at[pl.ds(2 * i, 2)], grecv.at[i]
        ).wait()
        return carry

    row_of = lax.broadcasted_iota(jnp.int32, (BLOCK, LANES), 0)
    lane_of = lax.broadcasted_iota(jnp.int32, (BLOCK, LANES), 1)
    inside = lane_of >= row_of

    def select(p, carry):
        tiles_ref[p] = arrived[places[p]]
        return carry

    share = pltpu.make_async_remote_copy(
        src_ref=tiles_ref.at[0:patches],
        dst_ref=tiles_ref.at[patches : 2 * patches],
        send_sem=psend,
        recv_sem=precv,
        device_id=(z, partner),
        device_id_type=MESH,
    )

    def build(p, carry):
        tile = tiles_ref[p].astype(jnp.float32)
        at = pl.multiple_of(p * BLOCK, BLOCK)
        for c in range(2):
            before = jnp.zeros((BLOCK, LANES), jnp.float32)
            for m in range(tiles + 1):
                if m < tiles:
                    row = tile[c : c + 1, m * LANES : (m + 1) * LANES]
                    turned = pltpu.roll(
                        jnp.broadcast_to(row, (BLOCK, LANES)), 0, 1, stride=1, stride_axis=0
                    )
                else:
                    turned = jnp.zeros((BLOCK, LANES), jnp.float32)
                block = jnp.where(inside, turned, before)
                before = turned
                start = c * width + m * LANES
                band[pl.ds(at, BLOCK), start : start + LANES] = block.astype(jnp.bfloat16)
        return carry

    zrelay(1, (2,))
    zrelay(3, (6, 4))
    lax.fori_loop(0, npd, gwait, 0)
    lax.fori_loop(0, patches, select, 0)
    share.start()
    lax.fori_loop(0, patches, build, 0)
    zrelay(4, (5,))
    zrelay(6, (8, 7))
    share.wait_recv()
    lax.fori_loop(patches, 2 * patches, build, 0)

    sub = lax.broadcasted_iota(jnp.int32, (8, out_len), 0)
    pad = jnp.zeros((8, LANES), jnp.float32)

    def rcopy(slot):
        chip = chip_of(slot)
        return chip, pltpu.make_async_remote_copy(
            src_ref=part.at[slot],
            dst_ref=recv.at[my_chip],
            send_sem=rsend.at[slot],
            recv_sem=rrecv.at[my_chip],
            device_id=(z, 2 * chip + core),
            device_id_type=MESH,
        )

    def chip_of(slot):
        if slot == 0:
            return z
        k = ARRIVAL[(slot - 1) // 2]
        return lax.rem(z + (nz - k if slot % 2 else k), nz)

    def compute(first, last):
        count = last - first
        left = gath[first:last].reshape(count * rows, 2 * depth)
        step = 256
        for n in range(0, 2 * width, step):
            prod[0 : count * rows, n : n + step] = jnp.dot(
                left, band[:, n : n + step], preferred_element_type=jnp.float32
            )
        for slot in range(first, last):
            base = (slot - first) * rows
            sums, turned = [], []
            for c in range(2):
                low, high = [
                    prod[base + 8 * i : base + 8 * i + 8, c * width : (c + 1) * width]
                    for i in range(2)
                ]
                total = jnp.concatenate([low, pad], 1) + jnp.concatenate([pad, high], 1)
                sums.append(total)
                turned.append(pltpu.roll(total, 2 * BLOCK, 1))
            both = jnp.where(sub < 4, sums[0], pltpu.roll(sums[1], 4, 0)) + jnp.where(
                sub < 4, pltpu.roll(turned[0], 4, 0), turned[1]
            )
            result = both + pltpu.roll(pltpu.roll(both, BLOCK, 1), 6, 0)
            part[slot, 0:2] = result[0:2]
            part[slot, 2:4] = result[4:6]
            chip, copy = rcopy(slot)

            @pl.when(chip != my_chip)
            def _():
                copy.start()

            @pl.when(chip == my_chip)
            def _():
                pltpu.make_async_copy(part.at[slot], recv.at[my_chip], rrecv.at[my_chip]).start()

    def both(k):
        zwait(k, 0)
        zwait(k, 1)

    swap.wait_recv()
    both(2)
    compute(0, 7)
    both(5)
    compute(7, 13)
    both(7)
    both(8)
    compute(13, 16)

    def rwait(i, carry):
        pltpu.make_async_copy(part.at[i], recv.at[i], rrecv.at[i]).wait()
        return carry

    lax.fori_loop(0, nz, rwait, 0)
    total = jnp.sum(recv[...], axis=0)
    for v in range(2):
        for c in range(2):
            out_ref[v, c : c + 1] = total[2 * c + v : 2 * c + v + 1]

    swap.wait_send()
    share.wait_send()
    for direction in (1, -1):
        for k in range(1, reach[direction] + 1):
            for half in range(2):
                zcopy(direction, k, half).wait_send()

    def gdrain(i, carry):
        @pl.when(i != me)
        def _():
            gcopy(i).wait_send()

        return carry

    lax.fori_loop(0, npd, gdrain, 0)
    for slot in range(nz):
        chip, copy = rcopy(slot)

        @pl.when(chip != my_chip)
        def _():
            copy.wait_send()


def local(nz, npd, slip_rates, green_tiles, patch_slot):
    patches, own_v, samples = slip_rates.shape
    lags = green_tiles.shape[3]
    blocks = samples // BLOCK
    assert own_v == 4 and blocks == 8 and npd == 2 * nz and nz == 16
    rows, depth = blocks * 2, patches * BLOCK
    chunk = (
        slip_rates.reshape(patches, 2, 2, blocks, BLOCK)
        .transpose(1, 3, 2, 0, 4)
        .reshape(2, rows, depth)
    )
    width, out_len = lags + LANES, lags + samples
    vmem = pl.BlockSpec(memory_space=pltpu.VMEM)
    hbm = pl.BlockSpec(memory_space=pltpu.HBM)
    dma = pltpu.SemaphoreType.DMA
    result = pl.pallas_call(
        functools.partial(kernel, nz, npd),
        out_shape=jax.ShapeDtypeStruct((2, 2, out_len), jnp.float32),
        in_specs=[hbm, vmem, hbm],
        out_specs=vmem,
        scratch_shapes=[
            pltpu.SMEM(patch_slot.shape, jnp.int32),
            pltpu.SMEM((patches,), jnp.int32),
            pltpu.VMEM(green_tiles.shape[1:], jnp.bfloat16),
            pltpu.VMEM((nz, rows, 2 * depth), jnp.bfloat16),
            pltpu.VMEM((2 * npd, 2, lags), jnp.bfloat16),
            pltpu.VMEM((2 * npd, 2, lags), jnp.bfloat16),
            pltpu.VMEM((2 * patches, 2, lags), jnp.bfloat16),
            pltpu.VMEM((2 * depth, 2 * width), jnp.bfloat16),
            pltpu.VMEM((7 * rows, 2 * width), jnp.float32),
            pltpu.VMEM((nz, 4, out_len), jnp.float32),
            pltpu.VMEM((nz, 4, out_len), jnp.float32),
            dma((2,)), dma((nz, 2)), dma((nz, 2)), dma((npd,)), dma((npd,)),
            dma, dma, dma((nz,)), dma((nz,)),
        ],
        compiler_params=pltpu.CompilerParams(
            collective_id=0, has_side_effects=True, vmem_limit_bytes=16 * 1024 * 1024
        ),
    )(pltpu.with_memory_space_constraint(patch_slot, pltpu.HBM), chunk, pltpu.with_memory_space_constraint(green_tiles[0], pltpu.HBM))
    return result[None]


def solution(mesh):
    in_specs = (P("patch", "site", None), P("site", "patch", None, None), P())
    out_specs = P("site", "patch", None, None)
    return jax.shard_map(
        functools.partial(local, mesh.shape["site"], mesh.shape["patch"]),
        mesh=mesh, in_specs=in_specs, out_specs=out_specs, check_vma=False,
    )
```

time: 41.9 us -> 41.2 us (0.983)
  local copies, waits for them, and re-layouts: 2.45 us -> 1.71 us
    unnamed x5 -> x1, local copies, waits for them, and re-layouts: 1.35 us -> 0.61 us
where the time goes in v3:
time: 41.2 us; the launch traced here: 41 us
  Pallas kernels  39.2 us (95%)
  local copies, waits for them, and re-layouts  1.71 us (4%)
    pallas_call x1, Pallas kernels, local(): pl.pallas_call(functools.partial(kernel, nz, npd), out_shape=jax.ShapeDty...  39.2 us
    reshape x2, local copies, waits for them, and re-layouts, local(): slip_rates.reshape(patches, 2, 2, blocks, BLOCK).transpose(1, 3, 2, 0, 4)  0.95 us

profile of v3, /device:TPU:4, one launch (start us, length us, event | category | flops | bytes accessed | tf_op | source)
XLA Modules:
  0.0 41.0 jit_solution(17019444712407114512)
XLA Ops:
  0.0 0.9 %reshape.6 = bf16[16,2,2,8,32]{4,3,2,1,0:T(8,128)(2,1)S(1)} reshape(bf16[16,4,256]{2,1,0:T(4,128)(2,1)} %param.3) | data formatting | bytes 65536 | tf_op jit(solution)/shard_map/reshape | solution.py:336
  0.9 0.1 copy.6
  1.0 0.2 reshape.7.slip_ref
  1.1 39.2 %shard_map.37 = f32[2,2,1280]{2,1,0:T(2,128)S(1)} custom-call(s32[512]{0:T(512)} %slots_hbm.1, bf16[2,16,512]{2,1,0:T(8,128)(2,1)S(1)} %reshape.7.slip_ref, bf16[32,2,1024]{2,1,0:T(2,128)(2,1)} %bitcast.9), custom_call_target="tpu_custom_call" | custom-call | tf_op jit(solution)/shard_map/pallas_call | solution.py:344
  40.4 0.6 %copy.8 = f32[1,2,2,1280]{3,2,1,0:T(2,128)} copy(f32[1,2,2,1280]{3,2,1,0:T(2,128)S(1)} %bitcast.7) | data formatting | bytes 40960

commit v4 on v3

--- a/solution.py
+++ b/solution.py
@@ -219,11 +219,11 @@
     lax.fori_loop(0, npd, gwait, 0)
     lax.fori_loop(0, patches, select, 0)
     share.start()
-    lax.fori_loop(0, patches, build, 0)
+    lax.fori_loop(0, patches, build, 0, unroll=4)
     zrelay(4, (5,))
     zrelay(6, (8, 7))
     share.wait_recv()
-    lax.fori_loop(patches, 2 * patches, build, 0)
+    lax.fori_loop(patches, 2 * patches, build, 0, unroll=4)
 
     sub = lax.broadcasted_iota(jnp.int32, (8, out_len), 0)
     pad = jnp.zeros((8, LANES), jnp.float32)

time: 41.2 us -> 40.3 us (0.978)
  Pallas kernels: 39.2 us -> 38.4 us
    pallas_call x1, Pallas kernels: 39.2 us -> 38.4 us  [local(): pl.pallas_call(functools.partial(kernel, nz, npd), out_shape=jax.ShapeDty...]
where the time goes in v4:
time: 40.3 us; the launch traced here: 40.1 us
  Pallas kernels  38.4 us (95%)
  local copies, waits for them, and re-layouts  1.71 us (4%)
    pallas_call x1, Pallas kernels, local(): pl.pallas_call(functools.partial(kernel, nz, npd), out_shape=jax.ShapeDty...  38.4 us
    reshape x2, local copies, waits for them, and re-layouts, local(): slip_rates.reshape(patches, 2, 2, blocks, BLOCK).transpose(1, 3, 2, 0, 4)  0.95 us

profile of v4, /device:TPU:4, one launch (start us, length us, event | category | flops | bytes accessed | tf_op | source)
XLA Modules:
  0.0 40.1 jit_solution(1591201508795936725)
XLA Ops:
  0.0 0.9 %reshape.6 = bf16[16,2,2,8,32]{4,3,2,1,0:T(8,128)(2,1)S(1)} reshape(bf16[16,4,256]{2,1,0:T(4,128)(2,1)} %param.3) | data formatting | bytes 65536 | tf_op jit(solution)/shard_map/reshape | solution.py:336
  0.9 0.1 copy.6
  1.0 0.2 reshape.7.slip_ref
  1.1 38.4 %shard_map.37 = f32[2,2,1280]{2,1,0:T(2,128)S(1)} custom-call(s32[512]{0:T(512)} %slots_hbm.1, bf16[2,16,512]{2,1,0:T(8,128)(2,1)S(1)} %reshape.7.slip_ref, bf16[32,2,1024]{2,1,0:T(2,128)(2,1)} %bitcast.9), custom_call_target="tpu_custom_call" | custom-call | tf_op jit(solution)/shard_map/pallas_call | solution.py:344
  39.5 0.6 %copy.8 = f32[1,2,2,1280]{3,2,1,0:T(2,128)} copy(f32[1,2,2,1280]{3,2,1,0:T(2,128)S(1)} %bitcast.7) | data formatting | bytes 40960
